TPU v7x, 512 devices: a whole 4x4x16 slice. The times are simulated.
512 devices in a mesh: front: 128 (over x, z, core), chain: 4 (over y).
Axes of the slice: x: 4, y: 4, z: 16, core: 2. Of those that a mesh axis runs over, the one named last changes fastest.
Arguments:
- rhs: float32 [131072, 128], P(('front', 'chain')), may hold values from -6 to 6
- child_blocks: bfloat16 [45056, 128, 128], P(('front', 'chain')), may hold values from -4 to 4
- dest_front: int32 [45056, 1], P(('front', 'chain')), may hold values from 0 to 127; in each aligned block of 88 rows (0 to 87, 88 to 175, ...) at most 2 rows name the same one
- dest_place: int32 [45056], P(('front', 'chain')), may hold values from -4 to 23
- front_pivots: int32 [128], P('front'), may hold values from 512 to 1024, as said below
- diag_inv: float32 [131072, 256], P(('front', 'chain')), as said below
- lower_factor: bfloat16 [131072, 768], P(('front', 'chain')), may hold values from -0.1875 to 0.1875
- update_factor: bfloat16 [262144, 1024], P(('front', 'chain')), may hold values from -0.1875 to 0.1875
Outputs:
- solution: float32 [131072, 128], P(('front', 'chain'))
- update_out: float32 [262144, 128], P(('front', 'chain'))
Inputs may be any that keep to these rules, and one draw needn't show every extreme that they name: `dest_front`: at most 2 of the 88 blocks of one device go to one front, and that many do in every draw. `front_pivots`: pivot rows at or beyond this count are padding and solve to zero; some front has all 1024. `diag_inv`: each 256 by 256 block is lower triangular with its diagonal between 0.4 and 1.6.
All inputs are finite; a program needn't handle non-finite values.
Results may differ from a plain program's by a relative error of at most 0.0027.
Values may be sent and summed in bfloat16 or wider, within the bound.
No kernel may reach another device: no remote copies, remote signals or barrier semaphores. Data moves between devices by JAX's collectives and lax.ppermute only.
A program may use at most 64 MiB of HBM per device.

v0:
```python
import jax
import jax.numpy as jnp
from jax import lax
from jax.sharding import PartitionSpec as P

BR = 128


def broadcast(value, axis, source):
    kept = jnp.where(lax.axis_index(axis) == source, value, 0).astype(value.dtype)
    return lax.psum(kept, axis)


def slot_table(blocks, fronts, places, dest_count, slot_width):
    block_count = fronts.shape[0]
    sequence = jnp.arange(block_count, dtype=jnp.int32)
    earlier = (fronts[None, :] == fronts[:, None]) & (sequence[None, :] < sequence[:, None])
    rank_of = jnp.sum(earlier.astype(jnp.int32), axis=1)
    target = fronts * slot_width + rank_of
    source = jnp.full((dest_count * slot_width,), block_count, jnp.int32).at[target].set(sequence)
    slot_data = jnp.take(blocks, source, axis=0, mode="fill", fill_value=0)
    labels = jnp.take(places, source, axis=0, mode="fill", fill_value=-1)
    return (
        slot_data.reshape((dest_count, slot_width) + blocks.shape[1:]),
        labels.reshape(dest_count, slot_width),
    )


def assemble(slot_data, labels, piv_blocks, upd_blocks, owners):
    flattened = slot_data.reshape((-1,) + slot_data.shape[2:])
    tag_list = labels.reshape(-1)
    per_owner = piv_blocks + upd_blocks
    first_update = piv_blocks * owners
    update_index = tag_list - first_update
    placed = jnp.where(
        tag_list < first_update,
        tag_list // piv_blocks * per_owner + tag_list % piv_blocks,
        update_index // upd_blocks * per_owner + piv_blocks + update_index % upd_blocks,
    )
    placed = jnp.where(tag_list < 0, -1, placed)
    row_ids = jnp.arange(owners * per_owner, dtype=jnp.int32)
    onehot = (placed[None, :] == row_ids[:, None]).astype(jnp.bfloat16)
    return jnp.einsum("km,mrs->krs", onehot, flattened, preferred_element_type=jnp.float32)


def body(
    rhs, child_blocks, dest_front, dest_place, front_pivots, diag_inv, lower_factor, update_factor
):
    owners = lax.axis_size("chain")
    front_count = lax.axis_size("front")
    chain_at = lax.axis_index("chain")
    piv_rows = rhs.shape[0]
    upd_rows = update_factor.shape[0]
    source_width = rhs.shape[1]
    piv_blocks = piv_rows // BR
    upd_blocks = upd_rows // BR
    per_device = child_blocks.shape[0]
    capacity = max(2, (per_device + front_count - 1) // front_count * 2)
    slot_data, labels = slot_table(
        child_blocks, dest_front[:, 0], dest_place, front_count, capacity
    )
    received, received_labels = (
        lax.all_to_all(slot_data, "front", split_axis=0, concat_axis=0, tiled=True),
        lax.all_to_all(labels, "front", split_axis=0, concat_axis=0, tiled=True),
    )
    merged = assemble(received, received_labels, piv_blocks, upd_blocks, owners)
    owned = lax.psum_scatter(merged, "chain", scatter_dimension=0, tiled=True)
    pivot_rhs = rhs + owned[:piv_blocks].reshape(piv_rows, source_width)
    update_start = owned[piv_blocks:].reshape(upd_rows, source_width)
    positions = chain_at * piv_rows + jnp.arange(piv_rows, dtype=jnp.int32)
    live_rows = (positions < front_pivots[0]).astype(jnp.float32)[:, None]
    running = pivot_rhs
    updates = update_start
    solved = jnp.zeros_like(pivot_rhs)
    for section in range(owners):
        candidate = live_rows * jnp.dot(diag_inv, running, precision=lax.Precision.HIGHEST)
        solved = jnp.where(chain_at == section, candidate, solved)
        solved_bf = broadcast(candidate.astype(jnp.bfloat16), "chain", section)
        advance_running = running
        advance_updates = updates
        if section < owners - 1:
            factor_block = lower_factor[:, section * piv_rows : (section + 1) * piv_rows]
            product = jnp.dot(factor_block, solved_bf, preferred_element_type=jnp.float32)
            advance_running = advance_running - jnp.where(chain_at > section, product, 0.0)
        update_block = update_factor[:, section * piv_rows : (section + 1) * piv_rows]
        advance_updates = advance_updates - jnp.dot(
            update_block, solved_bf, preferred_element_type=jnp.float32
        )
        running = advance_running
        updates = advance_updates
    return (solved, updates)


def solution(mesh):
    return jax.shard_map(
        body,
        mesh=mesh,
        in_specs=(
            P(("front", "chain"), None),
            P(("front", "chain"), None, None),
            P(("front", "chain"), None),
            P(("front", "chain")),
            P("front"),
            P(("front", "chain"), None),
            P(("front", "chain"), None),
            P(("front", "chain"), None),
        ),
        out_specs=(P(("front", "chain"), None), P(("front", "chain"), None)),
        check_vma=False,
    )
```

profile of v0, /device:TPU:2, one launch (start us, length us, event | category | flops | bytes accessed | tf_op | source)
XLA Modules:
  0.0 734.5 jit_solution(3407166581159611724)
XLA Ops:
  9.7 1.9 gather_fusion
  12.4 19.5 %all-to-all-start = ((s32[128,1,2]{2,1,0:T(1,128)}), s32[128,1,2]{2,1,0:T(1,128)S(1)}, u32[]{:S(2)}, u32[]{:S(2)}) async-start(s32[128,1,2]{2,1,0:T(1,128)} %bitcast.4), calls=%async_computation | async-start | bytes 131072 | tf_op jit(solution)/shard_map/all_to_all | solution.py:64
  32.1 8.4 %gather_fusion.1 = bf16[256,128,128]{2,1,0:T(8,128)(2,1)} fusion(bf16[88,128,128]{2,1,0:T(8,128)(2,1)S(1)} %copy-done, s32[1024]{0:T(1024)S(1)} %pad_clamp_fusion), kind=kCustom, calls=%fused_computation.1 | custom fusion | bytes 16778240 | tf_op jit(solution)/shard_map/jit(_take)/gather | solution.py:21
  40.5 7.3 broadcast_select_fusion
  47.8 16.3 %copy.40 = bf16[128,2,128,128]{3,1,2,0:T(2,128)(2,1)} copy(bf16[128,2,128,128]{3,2,1,0:T(8,128)(2,1)} %broadcast_select_fusion) | data formatting | bytes 16777216 | tf_op jit(solution)/shard_map/jit(_take)/select_n | solution.py:21
  64.1 16.7 %all-to-all-start.1 = ((bf16[128,2,128,128]{3,1,2,0:T(2,128)(2,1)}), bf16[128,2,128,128]{3,1,2,0:T(2,128)(2,1)}, u32[]{:S(2)}, u32[]{:S(2)}) async-start(bf16[128,2,128,128]{3,1,2,0:T(2,128)(2,1)} %copy.40), calls=%async_computation.1 | async-start | bytes 16777216 | tf_op jit(solution)/shard_map/all_to_all | solution.py:63
  82.3 364.7 %all-to-all-done.1 = bf16[128,2,128,128]{3,1,2,0:T(2,128)(2,1)} async-done(((bf16[128,2,128,128]{3,1,2,0:T(2,128)(2,1)}), bf16[128,2,128,128]{3,1,2,0:T(2,128)(2,1)}, u32[]{:S(2)}, u32[]{:S(2)}) %all-to-all-start.1) | async-done | bytes 8388640 | tf_op jit(solution)/shard_map/all_to_all | solution.py:63
  447.0 7.3 copy.41
  454.4 1.2 fusion.19
  455.5 1.5 copy.42
  458.0 28.3 %reduce-scatter.2.cloned.1.call-done = f32[6,128,128]{2,1,0:T(8,128)} async-done(((f32[24,128,128]{2,1,0:T(8,128)}), f32[6,128,128]{2,1,0:T(8,128)}) %reduce-scatter.2.cloned.1.call-update) | async-done | bytes 393232 | tf_op jit(solution)/shard_map/reduce_scatter | solution.py:67
  488.5 1.7 slice.41
  490.2 1.8 copy.45
  492.0 53.7 %all-reduce.5.cloned.1.call-done = bf16[256,128]{0,1:T(8,128)(2,1)} async-done(((bf16[256,128]{0,1:T(8,128)(2,1)}), bf16[256,128]{0,1:T(8,128)(2,1)}) %all-reduce.5.cloned.1.call-update) | async-done | bytes 65552 | tf_op jit(solution)/shard_map/psum | solution.py:11
  545.7 1.1 fusion.9
  547.9 2.0 fusion.3
  549.9 55.7 %all-reduce.7.cloned.1.call-done = bf16[256,128]{0,1:T(8,128)(2,1)} async-done(((bf16[256,128]{0,1:T(8,128)(2,1)}), bf16[256,128]{0,1:T(8,128)(2,1)}) %all-reduce.7.cloned.1.call-update) | async-done | bytes 65552 | tf_op jit(solution)/shard_map/psum | solution.py:11
  608.6 2.0 fusion.2
  610.6 55.2 %all-reduce.9.cloned.1.call-done = bf16[256,128]{0,1:T(8,128)(2,1)} async-done(((bf16[256,128]{0,1:T(8,128)(2,1)}), bf16[256,128]{0,1:T(8,128)(2,1)}) %all-reduce.9.cloned.1.call-update) | async-done | bytes 65552 | tf_op jit(solution)/shard_map/psum | solution.py:11
  665.7 1.2 fusion.5
  668.7 1.3 fusion.1
  670.7 1.7 copy.46
  672.3 53.6 %all-reduce.11.cloned.1.call-done = bf16[256,128]{0,1:T(8,128)(2,1)} async-done(((bf16[256,128]{0,1:T(8,128)(2,1)}), bf16[256,128]{0,1:T(8,128)(2,1)}) %all-reduce.11.cloned.1.call-update) | async-done | bytes 65552 | tf_op jit(solution)/shard_map/psum | solution.py:11
  725.9 1.2 fusion
  (50 shorter events, 14.7 us)
Async XLA Ops:
  7.2 25.0 %copy-start = (bf16[88,128,128]{2,1,0:T(8,128)(2,1)S(1)}, bf16[88,128,128]{2,1,0:T(8,128)(2,1)}, u32[]{:S(2)}) copy-start(bf16[88,128,128]{2,1,0:T(8,128)(2,1)} %param.9) | copy-start | bytes 8650756
  12.4 51.7 %all-to-all-start = ((s32[128,1,2]{2,1,0:T(1,128)}), s32[128,1,2]{2,1,0:T(1,128)S(1)}, u32[]{:S(2)}, u32[]{:S(2)}) async-start(s32[128,1,2]{2,1,0:T(1,128)} %bitcast.4), calls=%async_computation | async-start | bytes 131072 | tf_op jit(solution)/shard_map/all_to_all | solution.py:64
  64.1 382.9 %all-to-all-start.1 = ((bf16[128,2,128,128]{3,1,2,0:T(2,128)(2,1)}), bf16[128,2,128,128]{3,1,2,0:T(2,128)(2,1)}, u32[]{:S(2)}, u32[]{:S(2)}) async-start(bf16[128,2,128,128]{3,1,2,0:T(2,128)(2,1)} %copy.40), calls=%async_computation.1 | async-start | bytes 16777216 | tf_op jit(solution)/shard_map/all_to_all | solution.py:63
  80.8 405.6 %reduce-scatter.2.cloned.1.call-start = ((), (), s32[]{:S(2)}) async-start(), calls=%async_computation.3 | async-start | bytes 1966080 | tf_op jit(solution)/shard_map/reduce_scatter | solution.py:67
  454.3 2.9 copy-start.4
  454.3 33.1 %copy-start.1 = (f32[256,256]{1,0:T(8,128)S(1)}, f32[256,256]{1,0:T(8,128)}, u32[]{:S(2)}) copy-start(f32[256,256]{1,0:T(8,128)} %param.13) | copy-start | bytes 786436
  457.0 88.6 %all-reduce.5.cloned.1.call-start = ((), (), s32[]{:S(2)}) async-start(), calls=%async_computation.4 | async-start | bytes 131072 | tf_op jit(solution)/shard_map/psum | solution.py:11
  488.5 117.2 %all-reduce.7.cloned.1.call-start = ((), (), s32[]{:S(2)}) async-start(), calls=%async_computation.5 | async-start | bytes 131072 | tf_op jit(solution)/shard_map/psum | solution.py:11
  547.9 117.8 %all-reduce.9.cloned.1.call-start = ((), (), s32[]{:S(2)}) async-start(), calls=%async_computation.6 | async-start | bytes 131072 | tf_op jit(solution)/shard_map/psum | solution.py:11
  606.8 0.7 copy-start.3
  608.5 117.4 %all-reduce.11.cloned.1.call-start = ((), (), s32[]{:S(2)}) async-start(), calls=%async_computation.7 | async-start | bytes 131072 | tf_op jit(solution)/shard_map/psum | solution.py:11
  667.3 0.7 copy-start.2
Sparse Core Ops, SparseCore 0:
  457.2 29.1 reduce-scatter.1
  489.2 56.3 all-reduce.4
  548.6 57.0 all-reduce.6
  608.6 57.0 all-reduce.8
  668.8 57.0 all-reduce.10
where the time goes:
time: 735 us; the launch traced here: 734 us
  waiting for transfers between devices  611 us (83%)
  local copies, waits for them, and re-layouts  46.1 us (6%)
  starting transfers between devices  36.6 us (5%)
  between operations  14.7 us (2%)
  other arithmetic  13.1 us (2%)
  matrix products  12.8 us (2%)
    all_to_all x1, waiting for transfers between devices, body(): lax.all_to_all(slot_data, 'front', split_axis=0, concat_axis=0, tiled=True)  365 us
    psum x4, waiting for transfers between devices, broadcast(): return lax.psum(kept, axis)  218 us
    reduce_scatter x1, waiting for transfers between devices, body(): owned = lax.psum_scatter(merged, 'chain', scatter_dimension=0, tiled=True)  28.3 us
    all_to_all x1, starting transfers between devices, body(): lax.all_to_all(labels, 'front', split_axis=0, concat_axis=0, tiled=True)  19.5 us
    all_to_all x1, starting transfers between devices, body(): lax.all_to_all(slot_data, 'front', split_axis=0, concat_axis=0, tiled=True)  16.7 us
    select_n x1, local copies, waits for them, and re-layouts, slot_table(): slot_data = jnp.take(blocks, source, axis=0, mode='fill', fill_value=0)  16.3 us
  transfers between devices with their start and end apart: 7, of which 6 were waited for; matrix products, arithmetic and copies ran while one was open for 6% of the time, Pallas kernels for 0%

commit v1 on v0

--- a/solution.py
+++ b/solution.py
@@ -8,7 +8,10 @@
 
 def broadcast(value, axis, source):
     kept = jnp.where(lax.axis_index(axis) == source, value, 0).astype(value.dtype)
-    return lax.psum(kept, axis)
+    create_the_trails = lambda q_in, mesh_name: jnp.sum(
+        lax.all_gather(q_in, axis_name=mesh_name), 0
+    )
+    return create_the_trails(kept, axis)
 
 
 def slot_table(blocks, fronts, places, dest_count, slot_width):

time: 735 us -> 575 us (0.78)
  waiting for transfers between devices: 611 us -> 393 us
  blocking collectives: 0 us -> 51.7 us
    psum x4 -> x0, waiting for transfers between devices: 218 us -> none  [broadcast(): return lax.psum(kept, axis)]
    all_gather x0 -> x4, blocking collectives: none -> 51.7 us  [broadcast(): lax.all_gather(q_in, axis_name=mesh_name)]
  transfers between devices with their start and end apart: 7 -> 3, of which waited for: 6 -> 2; matrix products, arithmetic and copies ran while one was open for 6% -> 6% of each run, Pallas kernels for 0% -> 0%
where the time goes in v1:
time: 575 us; the launch traced here: 574 us
  waiting for transfers between devices  393 us (68%)
  blocking collectives  51.7 us (9%)
  local copies, waits for them, and re-layouts  48.8 us (8%)
  starting transfers between devices  36.4 us (6%)
  other arithmetic  17.1 us (3%)
  between operations  15 us (3%)
  matrix products  11.9 us (2%)
    all_to_all x1, waiting for transfers between devices, body(): lax.all_to_all(slot_data, 'front', split_axis=0, concat_axis=0, tiled=True)  365 us
    all_gather x4, blocking collectives, broadcast(): lax.all_gather(q_in, axis_name=mesh_name)  51.7 us
    reduce_scatter x1, waiting for transfers between devices, body(): owned = lax.psum_scatter(merged, 'chain', scatter_dimension=0, tiled=True)  28.5 us
    all_to_all x1, starting transfers between devices, body(): lax.all_to_all(labels, 'front', split_axis=0, concat_axis=0, tiled=True)  19.5 us
    all_to_all x1, starting transfers between devices, body(): lax.all_to_all(slot_data, 'front', split_axis=0, concat_axis=0, tiled=True)  16.7 us
    select_n x1, local copies, waits for them, and re-layouts, slot_table(): slot_data = jnp.take(blocks, source, axis=0, mode='fill', fill_value=0)  16.3 us
  transfers between devices with their start and end apart: 3, of which 2 were waited for; matrix products, arithmetic and copies ran while one was open for 6% of the time, Pallas kernels for 0%

profile of v1, /device:TPU:2, one launch (start us, length us, event | category | flops | bytes accessed | tf_op | source)
XLA Modules:
  0.0 574.0 jit_solution(17042543165254643444)
XLA Ops:
  9.7 1.9 gather_fusion
  12.4 19.5 %all-to-all-start = ((s32[128,1,2]{2,1,0:T(1,128)}), s32[128,1,2]{2,1,0:T(1,128)S(1)}, u32[]{:S(2)}, u32[]{:S(2)}) async-start(s32[128,1,2]{2,1,0:T(1,128)} %bitcast.4), calls=%async_computation | async-start | bytes 131072 | tf_op jit(solution)/shard_map/all_to_all | solution.py:67
  32.1 8.4 %gather_fusion.1 = bf16[256,128,128]{2,1,0:T(8,128)(2,1)} fusion(bf16[88,128,128]{2,1,0:T(8,128)(2,1)S(1)} %copy-done, s32[1024]{0:T(1024)S(1)} %pad_clamp_fusion), kind=kCustom, calls=%fused_computation.1 | custom fusion | bytes 16778240 | tf_op jit(solution)/shard_map/jit(_take)/gather | solution.py:24
  40.5 7.3 %broadcast_select_fusion = bf16[128,2,128,128]{3,2,1,0:T(8,128)(2,1)} fusion(bf16[128,2,128,128]{3,2,1,0:T(8,128)(2,1)} %bitcast.79, pred[128,2]{1,0:T(8,128)(4,1)S(1)} %broadcast_in_dim.50), kind=kLoop, calls=%fused_computation.3 | loop fusion | flops 4194304 | bytes 16777472 | tf_op jit(solution)/shard_map/jit(_take)/select_n | solution.py:24
  47.8 16.3 %copy.40 = bf16[128,2,128,128]{3,1,2,0:T(2,128)(2,1)} copy(bf16[128,2,128,128]{3,2,1,0:T(8,128)(2,1)} %broadcast_select_fusion) | data formatting | bytes 16777216 | tf_op jit(solution)/shard_map/jit(_take)/select_n | solution.py:24
  64.0 16.7 %all-to-all-start.1 = ((bf16[128,2,128,128]{3,1,2,0:T(2,128)(2,1)}), bf16[128,2,128,128]{3,1,2,0:T(2,128)(2,1)}, u32[]{:S(2)}, u32[]{:S(2)}) async-start(bf16[128,2,128,128]{3,1,2,0:T(2,128)(2,1)} %copy.40), calls=%async_computation.1 | async-start | bytes 16777216 | tf_op jit(solution)/shard_map/all_to_all | solution.py:66
  82.4 364.5 %all-to-all-done.1 = bf16[128,2,128,128]{3,1,2,0:T(2,128)(2,1)} async-done(((bf16[128,2,128,128]{3,1,2,0:T(2,128)(2,1)}), bf16[128,2,128,128]{3,1,2,0:T(2,128)(2,1)}, u32[]{:S(2)}, u32[]{:S(2)}) %all-to-all-start.1) | async-done | bytes 8388640 | tf_op jit(solution)/shard_map/all_to_all | solution.py:66
  447.0 7.3 %copy.41 = bf16[128,2,128,128]{3,1,0,2:T(2,128)(2,1)S(1)} copy(bf16[128,2,128,128]{3,1,2,0:T(2,128)(2,1)} %all-to-all-done.1) | data formatting | bytes 16777216 | tf_op jit(solution)/shard_map/all_to_all | solution.py:66
  455.5 1.4 copy.42
  457.8 28.5 %reduce-scatter.2.cloned.1.call-done = f32[6,128,128]{2,1,0:T(8,128)} async-done(((f32[24,128,128]{2,1,0:T(8,128)}), f32[6,128,128]{2,1,0:T(8,128)}) %reduce-scatter.2.cloned.1.call-update) | async-done | bytes 393232 | tf_op jit(solution)/shard_map/reduce_scatter | solution.py:70
  487.8 13.2 %all-gather = bf16[1024,128]{0,1:T(8,128)(2,1)} all-gather(bf16[256,128]{0,1:T(8,128)(2,1)S(1)} %select_bitcast_fusion.4), channel_id=2, replica_groups=mesh['front'=128,'chain'=4] {'chain'}, dimensions={0}, use_global_device_ids=true | all-gather | bytes 327680 | tf_op jit(solution)/shard_map/all_gather | solution.py:12
  501.0 1.8 reshape.176
  502.9 1.9 reduce_sum.61
  506.3 13.0 %all-gather.1 = bf16[1024,128]{0,1:T(8,128)(2,1)} all-gather(bf16[256,128]{0,1:T(8,128)(2,1)S(1)} %select_bitcast_fusion.3), channel_id=3, replica_groups=mesh['front'=128,'chain'=4] {'chain'}, dimensions={0}, use_global_device_ids=true | all-gather | bytes 327680 | tf_op jit(solution)/shard_map/all_gather | solution.py:12
  519.3 1.8 reshape.177
  521.2 1.9 reduce_sum.62
  525.3 13.0 %all-gather.2 = bf16[1024,128]{0,1:T(8,128)(2,1)} all-gather(bf16[256,128]{0,1:T(8,128)(2,1)S(1)} %select_bitcast_fusion.2), channel_id=4, replica_groups=mesh['front'=128,'chain'=4] {'chain'}, dimensions={0}, use_global_device_ids=true | all-gather | bytes 327680 | tf_op jit(solution)/shard_map/all_gather | solution.py:12
  538.3 1.8 reshape.178
  540.1 1.9 reduce_sum.63
  547.3 1.2 fusion.2
  548.5 1.9 fusion.1
  550.4 12.5 %all-gather.3 = bf16[1024,128]{0,1:T(8,128)(2,1)S(1)} all-gather(bf16[256,128]{0,1:T(8,128)(2,1)} %select_bitcast_fusion.1), channel_id=5, replica_groups=mesh['front'=128,'chain'=4] {'chain'}, dimensions={0}, use_global_device_ids=true | all-gather | bytes 327680 | tf_op jit(solution)/shard_map/all_gather | solution.py:12
  563.4 1.3 fusion
  565.5 1.7 copy.46
  (48 shorter events, 18.3 us)
Async XLA Ops:
  7.2 25.0 %copy-start = (bf16[88,128,128]{2,1,0:T(8,128)(2,1)S(1)}, bf16[88,128,128]{2,1,0:T(8,128)(2,1)}, u32[]{:S(2)}) copy-start(bf16[88,128,128]{2,1,0:T(8,128)(2,1)} %param.9) | copy-start | bytes 8650756
  12.4 51.6 %all-to-all-start = ((s32[128,1,2]{2,1,0:T(1,128)}), s32[128,1,2]{2,1,0:T(1,128)S(1)}, u32[]{:S(2)}, u32[]{:S(2)}) async-start(s32[128,1,2]{2,1,0:T(1,128)} %bitcast.4), calls=%async_computation | async-start | bytes 131072 | tf_op jit(solution)/shard_map/all_to_all | solution.py:67
  64.0 382.9 %all-to-all-start.1 = ((bf16[128,2,128,128]{3,1,2,0:T(2,128)(2,1)}), bf16[128,2,128,128]{3,1,2,0:T(2,128)(2,1)}, u32[]{:S(2)}, u32[]{:S(2)}) async-start(bf16[128,2,128,128]{3,1,2,0:T(2,128)(2,1)} %copy.40), calls=%async_computation.1 | async-start | bytes 16777216 | tf_op jit(solution)/shard_map/all_to_all | solution.py:66
  80.7 405.6 %reduce-scatter.2.cloned.1.call-start = ((), (), s32[]{:S(2)}) async-start(), calls=%async_computation.3 | async-start | bytes 1966080 | tf_op jit(solution)/shard_map/reduce_scatter | solution.py:70
  454.3 2.7 copy-start.3
  454.3 33.0 %copy-start.1 = (f32[256,256]{1,0:T(8,128)S(1)}, f32[256,256]{1,0:T(8,128)}, u32[]{:S(2)}) copy-start(f32[256,256]{1,0:T(8,128)} %param.13) | copy-start | bytes 786436
  524.2 0.7 copy-start.2
Sparse Core Ops, SparseCore 0:
  457.1 29.1 reduce-scatter.1
